TPU v7x, 32 devices: a whole 2x2x4 slice. The times are simulated.
32 devices in a mesh: layer: 8 (over y, x, core), dp: 4 (over z).
Axes of the slice: x: 2, y: 2, z: 4, core: 2. Of those that a mesh axis runs over, the one named last changes fastest.
Arguments:
- resid_in: bfloat16 [4, 128, 3584], P(None, 'dp'), may hold values from -6 to 6
- resid_out: bfloat16 [4, 128, 3584], P(None, ('layer', 'dp')), may hold values from -4 to 4
- encoder: bfloat16 [2, 3584, 32768], P(None, None, ('layer', 'dp')), may hold values from -0.09375 to 0.09375
- enc_bias: float32 [2, 32768], P(None, ('layer', 'dp')), may hold values from -3 to 3
- decoder: bfloat16 [5, 32768, 3584], P(None, ('layer', 'dp')), may hold values from -0.046875 to 0.046875
- active: int32 [4, 4, 32], replicated, may hold values from 0 to 127, all different within a row
Outputs:
- recon: bfloat16 [4, 128, 3584], P(None, ('layer', 'dp'))
- grad_encoder: bfloat16 [2, 3584, 32768], P(None, None, ('layer', 'dp'))
- grad_bias: float32 [2, 32768], P(None, ('layer', 'dp'))
- grad_decoder: bfloat16 [5, 32768, 3584], P(None, ('layer', 'dp'))
Inputs may be any that keep to these rules, and one draw needn't show every extreme that they name: Row active[l, n] lists 32 different blocks of layer l, active for tokens n * 32 to (n + 1) * 32 - 1; every block number appears in at least one row of active, counting the rows of all layers together (not necessarily in a row of every layer).
All inputs are finite; a program needn't handle non-finite values.
Results may differ from a plain program's by a relative error of at most 0.0059.
Values may be sent and summed in bfloat16 or wider, within the bound.
A program may use at most 192 MiB of HBM per device.

v0:
```python
import jax
import jax.numpy as jnp
from jax import lax
from jax.sharding import PartitionSpec as P

FEAT = 16384
BLOCK = 128
LAYERS = 4


def per_device(resid_in, resid_out, encoder, enc_bias, decoder, active):
    tok_dev = resid_in.shape[1]
    model_width = resid_in.shape[2]
    local_width = encoder.shape[2]
    dp_count = lax.axis_size("dp")
    all_count = lax.axis_size("layer") * dp_count
    device_rank = lax.axis_index("layer") * dp_count + lax.axis_index("dp")
    first_column = device_rank * local_width
    fold_side = first_column // FEAT
    offset = first_column - fold_side * FEAT
    targets = lax.all_gather(resid_out, ("layer", "dp"), axis=1, tiled=True)
    layer_ids = [fold_side, LAYERS - 1 - fold_side]
    picked = jnp.stack(
        [lax.dynamic_index_in_dim(resid_in, layer_id, 0, keepdims=False) for layer_id in layer_ids]
    )
    inputs = lax.all_gather(picked, "dp", axis=1, tiled=True)
    tokens = inputs.shape[1]
    pre_acts = (
        jnp.einsum("krd,kdf->krf", inputs, encoder, preferred_element_type=jnp.float32)
        + enc_bias[:, None, :]
    )
    block_ids = offset // BLOCK + jnp.arange(local_width // BLOCK, dtype=jnp.int32)
    block_masks = []
    for layer_id in layer_ids:
        listed = lax.dynamic_index_in_dim(active, layer_id, 0, keepdims=False)
        listed_hit = jnp.any(listed[:, :, None] == block_ids[None, None, :], axis=1).astype(
            jnp.float32
        )
        spread = jnp.broadcast_to(
            listed_hit[:, None, :, None], (listed_hit.shape[0], tok_dev, listed_hit.shape[1], BLOCK)
        )
        block_masks.append(spread.reshape(tokens, local_width))
    block_keep = jnp.stack(block_masks)
    positive = jnp.maximum(pre_acts, 0.0)
    feature_codes = (block_keep * positive * positive).astype(jnp.bfloat16)
    pair_table = []
    for pair_slot in range(decoder.shape[0]):
        second = pair_slot >= LAYERS - fold_side
        pair_table.append(
            (second.astype(jnp.int32), jnp.where(second, pair_slot - 1, fold_side + pair_slot))
        )
    decoded = jnp.zeros((LAYERS, tokens, model_width), jnp.float32)
    for pair_slot in range(decoder.shape[0]):
        source_slot, target_layer = pair_table[pair_slot]
        source_codes = lax.dynamic_index_in_dim(feature_codes, source_slot, 0, keepdims=False)
        decoded_part = jnp.dot(source_codes, decoder[pair_slot], preferred_element_type=jnp.float32)
        current = lax.dynamic_index_in_dim(decoded, target_layer, 0, keepdims=False)
        decoded = lax.dynamic_update_index_in_dim(decoded, current + decoded_part, target_layer, 0)
    totals = lax.psum(decoded, ("layer", "dp"))
    share = tokens // all_count
    recon = lax.dynamic_slice_in_dim(totals, device_rank * share, share, 1).astype(jnp.bfloat16)
    errors_all = (totals - targets.astype(jnp.float32)).astype(jnp.bfloat16)
    grad_parts = []
    back_codes = jnp.zeros((2, tokens, local_width), jnp.float32)
    for pair_slot in range(decoder.shape[0]):
        source_slot, target_layer = pair_table[pair_slot]
        source_codes = lax.dynamic_index_in_dim(feature_codes, source_slot, 0, keepdims=False)
        target_errors = lax.dynamic_index_in_dim(errors_all, target_layer, 0, keepdims=False)
        grad_parts.append(
            lax.dot_general(
                source_codes,
                target_errors,
                (((0,), (0,)), ((), ())),
                preferred_element_type=jnp.float32,
            ).astype(jnp.bfloat16)
        )
        pulled = lax.dot_general(
            target_errors,
            decoder[pair_slot],
            (((1,), (1,)), ((), ())),
            preferred_element_type=jnp.float32,
        )
        current = lax.dynamic_index_in_dim(back_codes, source_slot, 0, keepdims=False)
        back_codes = lax.dynamic_update_index_in_dim(back_codes, current + pulled, source_slot, 0)
    grad_decoder = jnp.stack(grad_parts)
    back_pre = (back_codes * block_keep * (2.0 * positive)).astype(jnp.bfloat16)
    grad_encoder = jnp.einsum(
        "krd,krf->kdf", inputs, back_pre, preferred_element_type=jnp.float32
    ).astype(jnp.bfloat16)
    grad_bias = jnp.sum(back_pre.astype(jnp.float32), axis=1)
    return (recon, grad_encoder, grad_bias, grad_decoder)


def solution(mesh):
    in_specs = (
        P(None, "dp", None),
        P(None, ("layer", "dp"), None),
        P(None, None, ("layer", "dp")),
        P(None, ("layer", "dp")),
        P(None, ("layer", "dp"), None),
        P(),
    )
    out_specs = (
        P(None, ("layer", "dp"), None),
        P(None, None, ("layer", "dp")),
        P(None, ("layer", "dp")),
        P(None, ("layer", "dp"), None),
    )
    return jax.shard_map(
        per_device, mesh=mesh, in_specs=in_specs, out_specs=out_specs, check_vma=False
    )
```

profile of v0, /device:TPU:0, one launch (start us, length us, event | category | flops | bytes accessed | tf_op | source)
XLA Modules:
  0.0 404.9 jit_solution(1773918791542335406)
XLA Ops:
  7.3 1.1 constant_dynamic-slice_fusion.9
  8.3 0.8 pad_maximum_fusion
  9.3 0.7 fusion.171
  10.9 43.4 %all-gather.3.cloned.1.call-done = bf16[2,128,3584]{2,1,0:T(8,128)(2,1)} async-done(((bf16[2,32,3584]{2,1,0:T(8,128)(2,1)}), bf16[2,128,3584]{2,1,0:T(8,128)(2,1)}) %all-gather.3.cloned.1.call-update) | async-done | bytes 1835024 | tf_op jit(solution)/shard_map/all_gather | solution.py:26
  54.2 8.0 %fusion.115 = (bf16[2,128,1024]{2,1,0:T(8,128)(2,1)S(1)}, f32[2,128,1024]{2,1,0:T(8,128)S(1)}) fusion(f32[2,128,1024]{2,1,0:T(8,128)S(1)} %constant_dynamic-update-slice_fusion, f32[2,1024]{1,0:T(2,128)S(1)} %copy-done.2, bf16[2,128,3584]{2,1,0:T(8,128)(2,1)} %all-gather.3.cloned.1.call-done, bf16[2,3584,1024]{2,1,0:T(8,128)(2,1)} %param.8), kind=kOutput, calls=%fused_computation.73 | convolution fusion | flops 1880358912 | bytes 19144704 | tf_op jit(solution)/shard_map/krd,kdf->krf/dot_general | solution.py:29
  62.2 3.9 broadcast_in_dim.52
  66.1 5.4 %fusion.33 = f32[4,128,3584]{2,1,0:T(8,128)} fusion(f32[4,128,3584]{2,1,0:T(8,128)} %broadcast_in_dim.52, s32[]{:T(128)S(6)} %select_n.104, bf16[5,1024,3584]{2,1,0:T(8,128)(2,1)} %param.10, bf16[2,128,1024]{2,1,0:T(8,128)(2,1)S(1)} %get-tuple-element.16, s32[]{:T(128)S(6)} %select_n.102), kind=kOutput, calls=%fused_computation.43 | convolution fusion | flops 939524096 | bytes 9437192 | tf_op jit(solution)/shard_map/dot_general | solution.py:56
  71.6 1.6 constant_dynamic-slice_fusion.7
  73.2 5.5 %fusion.42 = f32[4,128,3584]{2,1,0:T(8,128)} fusion(f32[4,128,3584]{2,1,0:T(8,128)} %fusion.33, s32[]{:T(128)S(6)} %select_n.106, bf16[5,1024,3584]{2,1,0:T(8,128)(2,1)} %param.10, f32[1,128,3584]{2,1,0:T(8,128)S(1)} %constant_dynamic-slice_fusion.7, bf16[2,128,1024]{2,1,0:T(8,128)(2,1)S(1)} %get-tuple-element.16, s32[]{:T(128)S(6)} %select_n.107), kind=kOutput, calls=%fused_computation.46 | convolution fusion | flops 939982848 | bytes 11272200 | tf_op jit(solution)/shard_map/dot_general | solution.py:56
  78.7 1.6 constant_dynamic-slice_fusion.6
  80.3 5.5 %fusion.51 = f32[4,128,3584]{2,1,0:T(8,128)} fusion(f32[4,128,3584]{2,1,0:T(8,128)} %fusion.42, s32[]{:T(128)S(6)} %select_n.109, bf16[5,1024,3584]{2,1,0:T(8,128)(2,1)} %param.10, f32[1,128,3584]{2,1,0:T(8,128)S(1)} %constant_dynamic-slice_fusion.6, bf16[2,128,1024]{2,1,0:T(8,128)(2,1)S(1)} %get-tuple-element.16, s32[]{:T(128)S(6)} %select_n.110), kind=kOutput, calls=%fused_computation.49 | convolution fusion | flops 939982848 | bytes 11272200 | tf_op jit(solution)/shard_map/dot_general | solution.py:56
  85.8 1.6 constant_dynamic-slice_fusion.4
  87.4 5.5 %fusion.60 = f32[4,128,3584]{2,1,0:T(8,128)} fusion(f32[4,128,3584]{2,1,0:T(8,128)} %fusion.51, s32[]{:T(128)S(6)} %select_n.112, bf16[5,1024,3584]{2,1,0:T(8,128)(2,1)} %param.10, f32[1,128,3584]{2,1,0:T(8,128)S(1)} %constant_dynamic-slice_fusion.4, bf16[2,128,1024]{2,1,0:T(8,128)(2,1)S(1)} %get-tuple-element.16, s32[]{:T(128)S(6)} %select_n.113), kind=kOutput, calls=%fused_computation.52 | convolution fusion | flops 939982848 | bytes 11272200 | tf_op jit(solution)/shard_map/dot_general | solution.py:56
  92.9 1.6 constant_dynamic-slice_fusion.3
  94.5 5.5 %fusion.69 = f32[4,128,3584]{2,1,0:T(8,128)} fusion(f32[4,128,3584]{2,1,0:T(8,128)} %fusion.60, s32[]{:T(128)S(6)} %select_n.115, bf16[5,1024,3584]{2,1,0:T(8,128)(2,1)} %param.10, f32[1,128,3584]{2,1,0:T(8,128)S(1)} %constant_dynamic-slice_fusion.3, bf16[2,128,1024]{2,1,0:T(8,128)(2,1)S(1)} %get-tuple-element.16, s32[]{:T(128)S(6)} %select_n.116), kind=kOutput, calls=%fused_computation.55 | convolution fusion | flops 939982848 | bytes 11272200 | tf_op jit(solution)/shard_map/dot_general | solution.py:56
  100.3 0.7 copy.19
  101.0 165.3 %all-reduce.2.cloned.1.call-done = f32[4,128,3584]{2,1,0:T(8,128)} async-done(((f32[4,128,3584]{2,1,0:T(8,128)}), f32[4,128,3584]{2,1,0:T(8,128)}) %all-reduce.2.cloned.1.call-update) | async-done | bytes 7340048 | tf_op jit(solution)/shard_map/psum | solution.py:59
  266.3 1.7 dynamic-slice_convert_fusion
  268.0 62.2 %all-gather.5.cloned.1.call-done = bf16[4,128,3584]{2,0,1:T(4,128)(2,1)} async-done(((bf16[4,4,3584]{2,0,1:T(4,128)(2,1)}), bf16[4,128,3584]{2,0,1:T(4,128)(2,1)}) %all-gather.5.cloned.1.call-update) | async-done | bytes 3670032 | tf_op jit(solution)/shard_map/all_gather | solution.py:21
  330.3 5.5 %subtract_convert_fusion = bf16[4,128,3584]{2,1,0:T(8,128)(2,1)S(1)} fusion(f32[4,128,3584]{2,1,0:T(8,128)} %all-reduce.2.cloned.1.call-done, bf16[4,128,3584]{2,0,1:T(4,128)(2,1)} %all-gather.5.cloned.1.call-done), kind=kLoop, calls=%fused_computation.31 | loop fusion | flops 5505024 | bytes 14680064 | tf_op jit(solution)/shard_map/convert_element_type | solution.py:62
  335.7 5.2 %bitcast_dynamic-update-slice_fusion.4 = bf16[5,1024,3584]{2,1,0:T(8,128)(2,1)} fusion(bf16[4,128,3584]{2,1,0:T(8,128)(2,1)S(1)} %subtract_convert_fusion, s32[]{:T(128)S(6)} %select_n.104, bf16[2,128,1024]{2,1,0:T(8,128)(2,1)S(1)} %get-tuple-element.16, s32[]{:T(128)S(6)} %select_n.102), kind=kOutput, calls=%fused_computation.10 | convolution fusion | flops 943194112 | bytes 8519688 | tf_op jit(solution)/shard_map/dot_general | solution.py:70
  340.9 5.1 %bitcast_dynamic-update-slice_fusion.3 = bf16[5,1024,3584]{2,1,0:T(8,128)(2,1)} fusion(bf16[5,1024,3584]{2,1,0:T(8,128)(2,1)} %bitcast_dynamic-update-slice_fusion.4, bf16[4,128,3584]{2,1,0:T(8,128)(2,1)S(1)} %subtract_convert_fusion, s32[]{:T(128)S(6)} %select_n.106, bf16[2,128,1024]{2,1,0:T(8,128)(2,1)S(1)} %get-tuple-element.16, s32[]{:T(128)S(6)} %select_n.107), kind=kOutput, calls=%fused_computation.9 | convolution fusion | flops 943194112 | bytes 8519688 | tf_op jit(solution)/shard_map/dot_general | solution.py:70
  346.0 5.1 %bitcast_dynamic-update-slice_fusion.2 = bf16[5,1024,3584]{2,1,0:T(8,128)(2,1)} fusion(bf16[5,1024,3584]{2,1,0:T(8,128)(2,1)} %bitcast_dynamic-update-slice_fusion.3, bf16[4,128,3584]{2,1,0:T(8,128)(2,1)S(1)} %subtract_convert_fusion, s32[]{:T(128)S(6)} %select_n.109, bf16[2,128,1024]{2,1,0:T(8,128)(2,1)S(1)} %get-tuple-element.16, s32[]{:T(128)S(6)} %select_n.110), kind=kOutput, calls=%fused_computation.8 | convolution fusion | flops 943194112 | bytes 8519688 | tf_op jit(solution)/shard_map/dot_general | solution.py:70
  351.2 5.1 %bitcast_dynamic-update-slice_fusion.1 = bf16[5,1024,3584]{2,1,0:T(8,128)(2,1)} fusion(bf16[5,1024,3584]{2,1,0:T(8,128)(2,1)} %bitcast_dynamic-update-slice_fusion.2, bf16[4,128,3584]{2,1,0:T(8,128)(2,1)S(1)} %subtract_convert_fusion, s32[]{:T(128)S(6)} %select_n.112, bf16[2,128,1024]{2,1,0:T(8,128)(2,1)S(1)} %get-tuple-element.16, s32[]{:T(128)S(6)} %select_n.113), kind=kOutput, calls=%fused_computation.7 | convolution fusion | flops 943194112 | bytes 8519688 | tf_op jit(solution)/shard_map/dot_general | solution.py:70
  356.3 5.1 %bitcast_dynamic-update-slice_fusion = bf16[5,1024,3584]{2,1,0:T(8,128)(2,1)} fusion(bf16[5,1024,3584]{2,1,0:T(8,128)(2,1)} %bitcast_dynamic-update-slice_fusion.1, bf16[4,128,3584]{2,1,0:T(8,128)(2,1)S(1)} %subtract_convert_fusion, s32[]{:T(128)S(6)} %select_n.115, bf16[2,128,1024]{2,1,0:T(8,128)(2,1)S(1)} %get-tuple-element.16, s32[]{:T(128)S(6)} %select_n.116), kind=kOutput, calls=%fused_computation.6 | convolution fusion | flops 943194112 | bytes 8519688 | tf_op jit(solution)/shard_map/dot_general | solution.py:70
  361.6 5.7 %fusion.76 = f32[2,128,1024]{2,1,0:T(8,128)S(1)} fusion(f32[2,128,1024]{2,1,0:T(8,128)S(1)} %broadcast.16, s32[]{:T(128)S(6)} %select_n.102, bf16[5,1024,3584]{2,1,0:T(8,128)(2,1)} %param.10, bf16[4,128,3584]{2,1,0:T(8,128)(2,1)S(1)} %subtract_convert_fusion, s32[]{:T(128)S(6)} %select_n.104), kind=kOutput, calls=%fused_computation.60 | convolution fusion | flops 939524096 | bytes 8781832 | tf_op jit(solution)/shard_map/dot_general | solution.py:77
  367.4 5.5 %fusion.85 = f32[2,128,1024]{2,1,0:T(8,128)S(1)} fusion(f32[2,128,1024]{2,1,0:T(8,128)S(1)} %fusion.76, s32[]{:T(128)S(6)} %select_n.107, bf16[5,1024,3584]{2,1,0:T(8,128)(2,1)} %param.10, bf16[4,128,3584]{2,1,0:T(8,128)(2,1)S(1)} %subtract_convert_fusion, s32[]{:T(128)S(6)} %select_n.106, f32[1,128,1024]{2,1,0:T(8,128)S(1)} %constant_dynamic-slice_fusion.2), kind=kOutput, calls=%fused_computation.63 | convolution fusion | flops 939655168 | bytes 9306120 | tf_op jit(solution)/shard_map/dot_general | solution.py:77
  373.0 5.5 %fusion.94 = f32[2,128,1024]{2,1,0:T(8,128)S(1)} fusion(f32[2,128,1024]{2,1,0:T(8,128)S(1)} %fusion.85, s32[]{:T(128)S(6)} %select_n.110, bf16[5,1024,3584]{2,1,0:T(8,128)(2,1)} %param.10, bf16[4,128,3584]{2,1,0:T(8,128)(2,1)S(1)} %subtract_convert_fusion, s32[]{:T(128)S(6)} %select_n.109, f32[1,128,1024]{2,1,0:T(8,128)S(1)} %constant_dynamic-slice_fusion.1), kind=kOutput, calls=%fused_computation.66 | convolution fusion | flops 939655168 | bytes 9306120 | tf_op jit(solution)/shard_map/dot_general | solution.py:77
  378.6 5.5 %fusion.103 = f32[2,128,1024]{2,1,0:T(8,128)S(1)} fusion(f32[2,128,1024]{2,1,0:T(8,128)S(1)} %fusion.94, s32[]{:T(128)S(6)} %select_n.113, bf16[5,1024,3584]{2,1,0:T(8,128)(2,1)} %param.10, bf16[4,128,3584]{2,1,0:T(8,128)(2,1)S(1)} %subtract_convert_fusion, s32[]{:T(128)S(6)} %select_n.112, f32[1,128,1024]{2,1,0:T(8,128)S(1)} %constant_dynamic-slice_fusion), kind=kOutput, calls=%fused_computation.69 | convolution fusion | flops 939655168 | bytes 9306120 | tf_op jit(solution)/shard_map/dot_general | solution.py:77
  384.2 5.7 %fusion.112 = f32[2,128,1024]{2,1,0:T(8,128)S(1)} fusion(f32[2,128,1024]{2,1,0:T(8,128)S(1)} %fusion.103, s32[]{:T(128)S(6)} %select_n.116, bf16[5,1024,3584]{2,1,0:T(8,128)(2,1)} %param.10, bf16[4,128,3584]{2,1,0:T(8,128)(2,1)S(1)} %subtract_convert_fusion, s32[]{:T(128)S(6)} %select_n.115, f32[1,128,1024]{2,1,0:T(8,128)S(1)} %constant_dynamic-slice_fusion.5), kind=kOutput, calls=%fused_computation.72 | convolution fusion | flops 939655168 | bytes 9306120 | tf_op jit(solution)/shard_map/dot_general | solution.py:77
  389.9 1.0 convert_reduce_fusion
  390.8 7.6 %convolution_convert_fusion = bf16[2,3584,1024]{2,1,0:T(8,128)(2,1)} fusion(bf16[2,128,3584]{2,1,0:T(8,128)(2,1)S(1)} %copy-done, bf16[2,128,1024]{2,1,0:T(8,128)(2,1)S(1)} %get-tuple-element.11), kind=kOutput, calls=%fused_computation | convolution fusion | flops 1886388224 | bytes 17039360 | tf_op jit(solution)/shard_map/krd,krf->kdf/dot_general | solution.py:87
  (27 shorter events, 1.4 us)
Async XLA Ops:
  7.2 47.1 %copy-start.2 = (f32[2,1024]{1,0:T(2,128)S(1)}, f32[2,1024]{1,0:T(2,128)}, u32[]{:S(2)}) copy-start(f32[2,1024]{1,0:T(2,128)} %param.9) | copy-start | bytes 24580
  7.2 47.0 %all-gather.3.cloned.1.call-start = ((), (), s32[]{:S(2)}) async-start(), calls=%async_computation | async-start | bytes 2293760 | tf_op jit(solution)/shard_map/all_gather | solution.py:26
  9.2 257.1 %all-reduce.2.cloned.1.call-start = ((), (), s32[]{:S(2)}) async-start(), calls=%async_computation.1 | async-start | bytes 14680064 | tf_op jit(solution)/shard_map/psum | solution.py:59
  94.5 5.8 %copy-start.1 = (bf16[4,4,3584]{2,1,0:T(4,128)(2,1)S(1)}, bf16[4,4,3584]{2,1,0:T(4,128)(2,1)}, u32[]{:S(2)}) copy-start(bf16[4,4,3584]{2,1,0:T(4,128)(2,1)} %param.7) | copy-start | bytes 344068
  100.0 230.2 %all-gather.5.cloned.1.call-start = ((), (), s32[]{:S(2)}) async-start(), calls=%async_computation.2 | async-start | bytes 3784704 | tf_op jit(solution)/shard_map/all_gather | solution.py:21
  384.2 6.6 %copy-start = (bf16[2,128,3584]{2,1,0:T(8,128)(2,1)S(1)}, bf16[2,128,3584]{2,1,0:T(8,128)(2,1)}, u32[]{:S(2)}) copy-start(bf16[2,128,3584]{2,1,0:T(8,128)(2,1)} %all-gather.3.cloned.1.call-done) | copy-start | bytes 5505028
Sparse Core Ops, SparseCore 0:
  10.1 44.0 all-gather.2
  100.2 166.0 all-reduce.1
  269.7 60.4 all-gather.4
where the time goes:
time: 406 us; the launch traced here: 405 us
  waiting for transfers between devices  271 us (67%)
  matrix products  96.6 us (24%)
  local copies, waits for them, and re-layouts  15.4 us (4%)
  between operations  14.1 us (3%)
  other arithmetic  7.55 us (2%)
    psum x1, waiting for transfers between devices, per_device(): totals = lax.psum(decoded, ('layer', 'dp'))  165 us
    all_gather x1, waiting for transfers between devices, per_device(): targets = lax.all_gather(resid_out, ('layer', 'dp'), axis=1, tiled=True)  62.2 us
    all_gather x1, waiting for transfers between devices, per_device(): inputs = lax.all_gather(picked, 'dp', axis=1, tiled=True)  43.4 us
    dot_general x5, matrix products, per_device(): lax.dot_general(target_errors, decoder[pair_slot], (((1,), (1,)), ((), ()...  28 us
    dot_general x5, matrix products, per_device(): jnp.dot(source_codes, decoder[pair_slot], preferred_element_type=jnp.floa...  27.3 us
    dot_general x5, matrix products, per_device(): lax.dot_general(source_codes, target_errors, (((0,), (0,)), ((), ())), pr...  25.7 us
  transfers between devices with their start and end apart: 3, of which 3 were waited for; matrix products, arithmetic and copies ran while one was open for 1% of the time, Pallas kernels for 0%

commit v1 on v0

--- a/solution.py
+++ b/solution.py
@@ -56,7 +56,7 @@
         decoded_part = jnp.dot(source_codes, decoder[pair_slot], preferred_element_type=jnp.float32)
         current = lax.dynamic_index_in_dim(decoded, target_layer, 0, keepdims=False)
         decoded = lax.dynamic_update_index_in_dim(decoded, current + decoded_part, target_layer, 0)
-    totals = lax.psum(decoded, ("layer", "dp"))
+    totals = lax.psum(lax.psum(decoded, "dp"), "layer")
     share = tokens // all_count
     recon = lax.dynamic_slice_in_dim(totals, device_rank * share, share, 1).astype(jnp.bfloat16)
     errors_all = (totals - targets.astype(jnp.float32)).astype(jnp.bfloat16)

time: 406 us -> 559 us (1.38)
  waiting for transfers between devices: 271 us -> 423 us
    psum x1 -> x2, waiting for transfers between devices: 165 us -> 368 us  [per_device(): totals = lax.psum(lax.psum(decoded, 'dp'), 'layer')]
    all_gather x1, waiting for transfers between devices: 62.2 us -> 11.6 us  [per_device(): targets = lax.all_gather(resid_out, ('layer', 'dp'), axis=1, tiled=True)]
  transfers between devices with their start and end apart: 3 -> 4, of which waited for: 3 -> 4; matrix products, arithmetic and copies ran while one was open for 1% -> 0% of each run, Pallas kernels for 0% -> 0%
where the time goes in v1:
time: 559 us; the launch traced here: 558 us
  waiting for transfers between devices  423 us (76%)
  matrix products  96.6 us (17%)
  between operations  15.5 us (3%)
  local copies, waits for them, and re-layouts  15.4 us (3%)
  other arithmetic  7.55 us (1%)
    psum x2, waiting for transfers between devices, per_device(): totals = lax.psum(lax.psum(decoded, 'dp'), 'layer')  368 us
    all_gather x1, waiting for transfers between devices, per_device(): inputs = lax.all_gather(picked, 'dp', axis=1, tiled=True)  43.4 us
    dot_general x5, matrix products, per_device(): lax.dot_general(target_errors, decoder[pair_slot], (((1,), (1,)), ((), ()...  28 us
    dot_general x5, matrix products, per_device(): jnp.dot(source_codes, decoder[pair_slot], preferred_element_type=jnp.floa...  27.3 us
    dot_general x5, matrix products, per_device(): lax.dot_general(source_codes, target_errors, (((0,), (0,)), ((), ())), pr...  25.7 us
    all_gather x1, waiting for transfers between devices, per_device(): targets = lax.all_gather(resid_out, ('layer', 'dp'), axis=1, tiled=True)  11.6 us
  transfers between devices with their start and end apart: 4, of which 4 were waited for; matrix products, arithmetic and copies ran while one was open for 0% of the time, Pallas kernels for 0%

profile of v1, /device:TPU:0, one launch (start us, length us, event | category | flops | bytes accessed | tf_op | source)
XLA Modules:
  0.0 558.3 jit_solution(5332202097280985552)
XLA Ops:
  8.1 1.1 constant_dynamic-slice_fusion.9
  9.2 0.8 pad_maximum_fusion
  10.1 0.7 fusion.171
  11.7 43.4 %all-gather.3.cloned.1.call-done = bf16[2,128,3584]{2,1,0:T(8,128)(2,1)} async-done(((bf16[2,32,3584]{2,1,0:T(8,128)(2,1)}), bf16[2,128,3584]{2,1,0:T(8,128)(2,1)}) %all-gather.3.cloned.1.call-update) | async-done | bytes 1835024 | tf_op jit(solution)/shard_map/all_gather | solution.py:26
  55.1 8.0 %fusion.115 = (bf16[2,128,1024]{2,1,0:T(8,128)(2,1)S(1)}, f32[2,128,1024]{2,1,0:T(8,128)S(1)}) fusion(f32[2,128,1024]{2,1,0:T(8,128)S(1)} %constant_dynamic-update-slice_fusion, f32[2,1024]{1,0:T(2,128)S(1)} %copy-done.2, bf16[2,128,3584]{2,1,0:T(8,128)(2,1)} %all-gather.3.cloned.1.call-done, bf16[2,3584,1024]{2,1,0:T(8,128)(2,1)} %param.8), kind=kOutput, calls=%fused_computation.73 | convolution fusion | flops 1880358912 | bytes 19144704 | tf_op jit(solution)/shard_map/krd,kdf->krf/dot_general | solution.py:29
  63.0 3.9 broadcast_in_dim.52
  67.0 5.4 fusion.33
  72.4 1.6 constant_dynamic-slice_fusion.7
  74.0 5.5 fusion.42
  79.5 1.6 constant_dynamic-slice_fusion.6
  81.1 5.5 fusion.51
  86.6 1.6 constant_dynamic-slice_fusion.4
  88.2 5.5 fusion.60
  93.7 1.6 constant_dynamic-slice_fusion.3
  95.4 5.5 fusion.69
  101.9 260.7 %all-reduce.3.cloned.1.call-done = f32[4,128,3584]{2,1,0:T(8,128)} async-done(((f32[4,128,3584]{2,1,0:T(8,128)}), f32[4,128,3584]{2,1,0:T(8,128)}) %all-reduce.3.cloned.1.call-update) | async-done | bytes 7340048 | tf_op jit(solution)/shard_map/psum | solution.py:59
  362.7 11.6 %all-gather.5.cloned.1.call-done = bf16[4,128,3584]{2,0,1:T(4,128)(2,1)} async-done(((bf16[4,4,3584]{2,0,1:T(4,128)(2,1)}), bf16[4,128,3584]{2,0,1:T(4,128)(2,1)}) %all-gather.5.cloned.1.call-update) | async-done | bytes 3670032 | tf_op jit(solution)/shard_map/all_gather | solution.py:21
  374.2 107.1 %all-reduce.5.cloned.1.call-done = f32[4,128,3584]{2,1,0:T(8,128)} async-done(((f32[4,128,3584]{2,1,0:T(8,128)}), f32[4,128,3584]{2,1,0:T(8,128)}) %all-reduce.5.cloned.1.call-update) | async-done | bytes 7340048 | tf_op jit(solution)/shard_map/psum | solution.py:59
  481.3 5.5 subtract_convert_fusion
  486.8 5.2 bitcast_dynamic-update-slice_fusion.4
  491.9 5.1 bitcast_dynamic-update-slice_fusion.3
  497.1 5.1 bitcast_dynamic-update-slice_fusion.2
  502.2 5.1 bitcast_dynamic-update-slice_fusion.1
  507.4 5.1 bitcast_dynamic-update-slice_fusion
  512.6 5.5 fusion.76
  518.2 5.7 %fusion.85 = f32[2,128,1024]{2,1,0:T(8,128)S(1)} fusion(f32[2,128,1024]{2,1,0:T(8,128)S(1)} %fusion.76, s32[]{:T(128)S(6)} %select_n.107, bf16[5,1024,3584]{2,1,0:T(8,128)(2,1)} %param.10, bf16[4,128,3584]{2,1,0:T(8,128)(2,1)S(1)} %subtract_convert_fusion, s32[]{:T(128)S(6)} %select_n.106, f32[1,128,1024]{2,1,0:T(8,128)S(1)} %constant_dynamic-slice_fusion.2), kind=kOutput, calls=%fused_computation.63 | convolution fusion | flops 939655168 | bytes 9306120 | tf_op jit(solution)/shard_map/dot_general | solution.py:77
  524.0 5.5 fusion.94
  529.6 5.5 fusion.103
  535.2 5.7 %fusion.112 = f32[2,128,1024]{2,1,0:T(8,128)S(1)} fusion(f32[2,128,1024]{2,1,0:T(8,128)S(1)} %fusion.103, s32[]{:T(128)S(6)} %select_n.116, bf16[5,1024,3584]{2,1,0:T(8,128)(2,1)} %param.10, bf16[4,128,3584]{2,1,0:T(8,128)(2,1)S(1)} %subtract_convert_fusion, s32[]{:T(128)S(6)} %select_n.115, f32[1,128,1024]{2,1,0:T(8,128)S(1)} %constant_dynamic-slice_fusion.5), kind=kOutput, calls=%fused_computation.72 | convolution fusion | flops 939655168 | bytes 9306120 | tf_op jit(solution)/shard_map/dot_general | solution.py:77
  540.9 1.0 convert_reduce_fusion
  541.9 7.6 %convolution_convert_fusion = bf16[2,3584,1024]{2,1,0:T(8,128)(2,1)} fusion(bf16[2,128,3584]{2,1,0:T(8,128)(2,1)S(1)} %copy-done, bf16[2,128,1024]{2,1,0:T(8,128)(2,1)S(1)} %get-tuple-element.11), kind=kOutput, calls=%fused_computation | convolution fusion | flops 1886388224 | bytes 17039360 | tf_op jit(solution)/shard_map/krd,krf->kdf/dot_general | solution.py:87
  549.4 1.7 dynamic-slice_convert_fusion
  (30 shorter events, 2.2 us)
Async XLA Ops:
  8.0 47.1 %copy-start.2 = (f32[2,1024]{1,0:T(2,128)S(1)}, f32[2,1024]{1,0:T(2,128)}, u32[]{:S(2)}) copy-start(f32[2,1024]{1,0:T(2,128)} %param.9) | copy-start | bytes 24580
  8.0 47.0 %all-gather.3.cloned.1.call-start = ((), (), s32[]{:S(2)}) async-start(), calls=%async_computation | async-start | bytes 2293760 | tf_op jit(solution)/shard_map/all_gather | solution.py:26
  10.0 352.6 %all-reduce.3.cloned.1.call-start = ((), (), s32[]{:S(2)}) async-start(), calls=%async_computation.1 | async-start | bytes 14680064 | tf_op jit(solution)/shard_map/psum | solution.py:59
  95.3 5.6 %copy-start.1 = (bf16[4,4,3584]{2,1,0:T(4,128)(2,1)S(1)}, bf16[4,4,3584]{2,1,0:T(4,128)(2,1)}, u32[]{:S(2)}) copy-start(bf16[4,4,3584]{2,1,0:T(4,128)(2,1)} %param.7) | copy-start | bytes 344068
  100.9 273.3 %all-gather.5.cloned.1.call-start = ((), (), s32[]{:S(2)}) async-start(), calls=%async_computation.3 | async-start | bytes 3784704 | tf_op jit(solution)/shard_map/all_gather | solution.py:21
  101.7 379.6 %all-reduce.5.cloned.1.call-start = ((), (), s32[]{:S(2)}) async-start(), calls=%async_computation.2 | async-start | bytes 14680064 | tf_op jit(solution)/shard_map/psum | solution.py:59
  535.2 6.6 %copy-start = (bf16[2,128,3584]{2,1,0:T(8,128)(2,1)S(1)}, bf16[2,128,3584]{2,1,0:T(8,128)(2,1)}, u32[]{:S(2)}) copy-start(bf16[2,128,3584]{2,1,0:T(8,128)(2,1)} %all-gather.3.cloned.1.call-done) | copy-start | bytes 5505028
Sparse Core Ops, SparseCore 0:
  11.0 44.0 all-gather.2
  101.0 261.5 all-reduce.2
  365.9 115.3 all-reduce.4
Sparse Core Ops, SparseCore 1:
  104.8 269.4 all-gather.4
